TPU v7x, 32 devices: a whole 2x2x4 slice. The times are simulated.
32 devices in a mesh: row: 4 (over z), col: 8 (over y, x, core).
Axes of the slice: x: 2, y: 2, z: 4, core: 2. Of those that a mesh axis runs over, the one named last changes fastest.
Arguments:
- ancestor_pivot: float32 [8, 512, 4, 1024], P(None, 'row', None, 'col'), as said below
- child_pivot: float32 [8, 512, 4, 1024], P(None, 'row', None, 'col'), as said below
- child_panel: float32 [8, 512, 4, 1024], P(None, 'row', None, 'col'), may hold values from -0.09375 to 0.09375
- block_pattern: int32 [32, 32], replicated, may hold values 0 or 1
Outputs:
- child_inverse: float32 [8, 512, 4, 1024], P(None, 'row', None, 'col')
Inputs may be any that keep to these rules, and one draw needn't show every extreme that they name: ancestor_pivot is an exactly symmetric 4096 x 4096 matrix. child_pivot is an exactly symmetric 4096 x 4096 matrix.
All inputs are finite; a program needn't handle non-finite values.
Results may differ from a plain program's by a relative error of at most 0.00005.
Values sent between devices are 32-bit elements; how exact they have to be, the bound alone decides.
A program may use at most 128 MiB of HBM per device.

v0:
```python
import jax
import jax.numpy as jnp
from jax import lax
from jax.sharding import PartitionSpec as P


def column_term(stationary, local_rows, piece):
    shaped = piece.reshape(local_rows, piece.shape[2], piece.shape[3])
    return jnp.einsum(
        "kcl,kn->cln",
        shaped,
        stationary,
        precision=lax.Precision.HIGHEST,
        preferred_element_type=jnp.float32,
    )


def local(ancestor_pivot, child_pivot, child_panel, block_pattern):
    anc_blocks = child_panel.shape[0]
    block_size = child_panel.shape[1]
    col_blocks = child_panel.shape[2]
    anc_col_blocks = ancestor_pivot.shape[2]
    child_rows = child_pivot.shape[0]
    row_count = lax.axis_size("row")
    col_count = lax.axis_size("col")
    row_index = lax.axis_index("row")
    col_index = lax.axis_index("col")
    local_rows = anc_blocks * block_size
    local_cols = col_blocks * block_size
    blocks = block_pattern.reshape(anc_blocks, row_count, col_blocks, col_count)
    local_mask = lax.dynamic_index_in_dim(blocks, row_index, 1, keepdims=False)
    local_mask = lax.dynamic_index_in_dim(local_mask, col_index, 2, keepdims=False)
    masked = child_panel * local_mask.astype(jnp.float32)[:, None, :, None]
    masked_flat = masked.reshape(local_rows, local_cols)
    panel_all = lax.all_gather(masked, "row", axis=1, tiled=True)
    panel_split = panel_all.reshape(anc_col_blocks, col_count * block_size, local_cols)
    segment = lax.all_gather(ancestor_pivot, "col", axis=3, tiled=True)
    length = segment.shape[3]
    weights = segment.reshape(local_rows, anc_col_blocks, length)
    product = jnp.einsum(
        "kcl,cln->kn",
        weights,
        panel_split,
        precision=lax.Precision.HIGHEST,
        preferred_element_type=jnp.float32,
    )
    product_blocks = product.reshape(anc_blocks, block_size, col_blocks, block_size)
    term = column_term(
        masked_flat, local_rows, lax.all_gather(product_blocks, "col", axis=3, tiled=True)
    )
    term = term.reshape(child_rows, row_count, block_size, local_cols)
    term = jnp.transpose(term, (1, 0, 2, 3)).reshape(
        row_count * child_rows * block_size, local_cols
    )
    summed = lax.psum_scatter(term, "row", scatter_dimension=0, tiled=True)
    return child_pivot + summed.reshape(child_rows, block_size, col_blocks, block_size)


def solution(mesh):
    return jax.shard_map(
        local,
        mesh=mesh,
        in_specs=(
            P(None, "row", None, "col"),
            P(None, "row", None, "col"),
            P(None, "row", None, "col"),
            P(),
        ),
        out_specs=P(None, "row", None, "col"),
        check_vma=False,
    )
```

profile of v0, /device:TPU:0, one launch (start us, length us, event | category | flops | bytes accessed | tf_op | source)
XLA Modules:
  0.0 626.5 jit_solution(12353932388971323393)
XLA Ops:
  6.5 0.0 all-gather.4.cloned.1.call-start
  6.5 0.8 reshape.28
  7.4 0.1 constant_dynamic-slice_fusion
  7.4 0.1 copy.15
  7.6 0.1 copy.9
  7.6 3.4 broadcast_multiply_fusion
  11.0 0.0 all-gather.4.cloned.1.call-update
  11.0 0.0 all-gather.6.cloned.1.call-start
  11.1 0.7 all-gather.6.cloned.1.call-update
  11.8 0.0 all-gather.8.cloned.1.call-start
  11.8 151.7 %all-gather.4.cloned.1.call-done = f32[8,512,4,128]{3,2,1,0:T(4,128)} async-done(((f32[8,128,4,128]{3,2,1,0:T(4,128)}), f32[8,512,4,128]{3,2,1,0:T(4,128)}) %all-gather.4.cloned.1.call-update) | async-done | bytes 8388624 | tf_op jit(solution)/shard_map/all_gather | solution.py:35
  163.5 10.5 %reshape.29 = f32[4,1024,512]{2,1,0:T(8,128)} reshape(f32[8,512,4,128]{3,2,1,0:T(4,128)} %all-gather.4.cloned.1.call-done) | data formatting | bytes 16777216 | tf_op jit(solution)/shard_map/reshape | solution.py:36
  174.0 82.6 %all-gather.6.cloned.1.call-done = f32[8,128,4,1024]{3,2,1,0:T(4,128)} async-done(((f32[8,128,4,128]{3,2,1,0:T(4,128)}), f32[8,128,4,1024]{3,2,1,0:T(4,128)}) %all-gather.6.cloned.1.call-update) | async-done | bytes 16777232 | tf_op jit(solution)/shard_map/all_gather | solution.py:37
  256.6 0.0 copy-start.1
  256.6 15.3 %copy.10 = f32[8,128,4,1024]{3,1,0,2:T(8,128)S(1)} copy(f32[8,128,4,1024]{3,2,1,0:T(4,128)} %all-gather.6.cloned.1.call-done) | data formatting | bytes 33554432 | tf_op jit(solution)/shard_map/all_gather | solution.py:37
  272.0 0.0 copy-done.1
  272.0 0.0 copy-start
  272.0 54.8 %convolution_bitcast_fusion.1 = f32[64,8,8,128]{3,1,2,0:T(8,128)S(1)} fusion(f32[4,1024,512]{2,1,0:T(8,128)S(1)} %copy-done.1, f32[1024,4,1024]{2,0,1:T(8,128)S(1)} %bitcast.29), kind=kOutput, calls=%fused_computation.2 | convolution fusion | flops 25769803776 | bytes 27262976 | tf_op jit(solution)/shard_map/kcl,cln->kn/dot_general | solution.py:40
  326.9 1.8 copy.16
  328.6 0.0 all-gather.8.cloned.1.call-update
  328.7 0.0 reduce-scatter.2.cloned.1.call-start
  328.7 0.0 copy-done
  328.7 1.8 reshape.37
  330.6 0.0 copy-start.2
  330.6 88.0 %all-gather.8.cloned.1.call-done = f32[8,128,4,1024]{1,0,3,2:T(8,128)} async-done(((f32[8,128,4,128]{1,0,3,2:T(8,128)}), f32[8,128,4,1024]{1,0,3,2:T(8,128)}) %all-gather.8.cloned.1.call-update) | async-done | bytes 16777232 | tf_op jit(solution)/shard_map/all_gather | solution.py:49
  418.5 18.0 %reshape.32 = f32[1024,4,1024]{0,2,1:T(8,128)} reshape(f32[8,128,4,1024]{1,0,3,2:T(8,128)} %all-gather.8.cloned.1.call-done) | data formatting | bytes 33554432 | tf_op jit(solution)/shard_map/reshape | solution.py:8
  436.5 0.0 copy-done.2
  436.5 29.1 %convolution_bitcast_fusion = f32[4,8,128,512]{3,2,0,1:T(8,128)S(1)} fusion(f32[8,4,128,1024]{3,2,1,0:T(8,128)} %bitcast.30, f32[1024,512,1,1]{1,0,2,3:T(8,128)S(1)} %copy-done.2), kind=kOutput, calls=%fused_computation | convolution fusion | flops 25769803776 | bytes 27262976 | tf_op jit(solution)/shard_map/kcl,kn->cln/dot_general | solution.py:9
  465.6 4.2 copy.12
  469.8 0.0 reduce-scatter.2.cloned.1.call-update
  469.9 144.8 %reduce-scatter.2.cloned.1.call-done = f32[1024,512]{1,0:T(8,128)} async-done(((f32[4096,512]{1,0:T(8,128)}), f32[1024,512]{1,0:T(8,128)}) %reduce-scatter.2.cloned.1.call-update) | async-done | bytes 2097168 | tf_op jit(solution)/shard_map/reduce_scatter | solution.py:55
  614.6 1.9 reshape.35
  616.6 3.5 add.19
  (1 shorter events, 0.0 us)
Async XLA Ops:
  6.5 157.0 %all-gather.4.cloned.1.call-start = ((), (), s32[]{:S(2)}) async-start(), calls=%async_computation.1 | async-start | bytes 10485760 | tf_op jit(solution)/shard_map/all_gather | solution.py:35
  11.0 245.6 %all-gather.6.cloned.1.call-start = ((), (), s32[]{:S(2)}) async-start(), calls=%async_computation.2 | async-start | bytes 18874368 | tf_op jit(solution)/shard_map/all_gather | solution.py:37
  11.8 406.8 %all-gather.8.cloned.1.call-start = ((), (), s32[]{:S(2)}) async-start(), calls=%async_computation.3 | async-start | bytes 18874368 | tf_op jit(solution)/shard_map/all_gather | solution.py:49
  256.6 15.4 %copy-start.1 = (f32[4,1024,512]{2,1,0:T(8,128)S(1)}, f32[4,1024,512]{2,1,0:T(8,128)}, u32[]{:S(2)}) copy-start(f32[4,1024,512]{2,1,0:T(8,128)} %reshape.29) | copy-start | bytes 25165828
  272.0 56.7 %copy-start = (f32[8,128,4,128]{3,2,1,0:T(4,128)S(1)}, f32[8,128,4,128]{3,2,1,0:T(4,128)}, u32[]{:S(2)}) copy-start(f32[8,128,4,128]{3,2,1,0:T(4,128)} %broadcast_multiply_fusion) | copy-start | bytes 6291460
  328.7 286.0 %reduce-scatter.2.cloned.1.call-start = ((), (), s32[]{:S(2)}) async-start(), calls=%async_computation.4 | async-start | bytes 10485760 | tf_op jit(solution)/shard_map/reduce_scatter | solution.py:55
  330.6 106.0 %copy-start.2 = (f32[1024,512,1,1]{1,0,2,3:T(8,128)S(1)}, f32[1024,512,1,1]{1,0,2,3:T(8,128)}, u32[]{:S(2)}) copy-start(f32[1024,512,1,1]{1,0,2,3:T(8,128)} %reshape.37) | copy-start | bytes 6291460
Sparse Core Ops, SparseCore 0:
  11.1 152.3 all-gather.3
  165.4 91.1 all-gather.5
  328.8 89.7 all-gather.7
  470.0 144.6 reduce-scatter.1
where the time goes:
time: 627 us
  waiting for transfers between devices  468 us (75%)
  matrix products  83.9 us (13%)
  local copies, waits for them, and re-layouts  54.7 us (9%)
  between operations  13.2 us (2%)
  other arithmetic  6.82 us (1%)
    all_gather x1, waiting for transfers between devices, local(): panel_all = lax.all_gather(masked, 'row', axis=1, tiled=True)  152 us
    reduce_scatter x1, waiting for transfers between devices, local(): summed = lax.psum_scatter(term, 'row', scatter_dimension=0, tiled=True)  145 us
    all_gather x1, waiting for transfers between devices, local(): lax.all_gather(product_blocks, 'col', axis=3, tiled=True)  88 us
    all_gather x1, waiting for transfers between devices, local(): segment = lax.all_gather(ancestor_pivot, 'col', axis=3, tiled=True)  82.6 us
    dot_general x1, matrix products, local(): jnp.einsum('kcl,cln->kn', weights, panel_split, precision=lax.Precision.H...  54.8 us
    dot_general x1, matrix products, column_term(): jnp.einsum('kcl,kn->cln', shaped, stationary, precision=lax.Precision.HIG...  29.1 us
    reshape x1, local copies, waits for them, and re-layouts, column_term(): shaped = piece.reshape(local_rows, piece.shape[2], piece.shape[3])  18 us
    all_gather x1, local copies, waits for them, and re-layouts, local(): segment = lax.all_gather(ancestor_pivot, 'col', axis=3, tiled=True)  15.3 us
  transfers between devices with their start and end apart: 4, of which 4 were waited for; matrix products, arithmetic and copies ran while one was open for 2% of the time, Pallas kernels for 0%

commit v1 on v0

--- a/solution.py
+++ b/solution.py
@@ -2,6 +2,7 @@
 import jax.numpy as jnp
 from jax import lax
 from jax.sharding import PartitionSpec as P
+from jax.lax import axis_index, axis_size, ppermute
 
 
 def column_term(stationary, local_rows, piece):
@@ -45,9 +46,28 @@
         preferred_element_type=jnp.float32,
     )
     product_blocks = product.reshape(anc_blocks, block_size, col_blocks, block_size)
-    term = column_term(
-        masked_flat, local_rows, lax.all_gather(product_blocks, "col", axis=3, tiled=True)
-    )
+
+    def convert_field_up(sheet, link_axis):
+        a_now, spare, t1 = (axis_size(link_axis), axis_index(link_axis), sheet.shape[3])
+        so_far_all = tuple(((kk, (kk + 1) % a_now) for kk in range(a_now)))
+        all_rows = tuple(((kk, (kk - 1) % a_now) for kk in range(a_now)))
+        x_next = jnp.zeros((*sheet.shape[:3], a_now * t1, *sheet.shape[4:]), sheet.dtype)
+        x_next = lax.dynamic_update_slice_in_dim(x_next, sheet, spare * t1, axis=3)
+        answer = base_arr = sheet
+        carry = a_now // 2
+        for c in range(1, carry + 1):
+            answer = ppermute(answer, link_axis, so_far_all)
+            x_next = lax.dynamic_update_slice_in_dim(
+                x_next, answer, (spare - c) % a_now * t1, axis=3
+            )
+            if c < a_now - carry:
+                base_arr = ppermute(base_arr, axis_name=link_axis, perm=all_rows)
+                x_next = lax.dynamic_update_slice_in_dim(
+                    x_next, base_arr, (spare + c) % a_now * t1, axis=3
+                )
+        return x_next
+
+    term = column_term(masked_flat, local_rows, convert_field_up(product_blocks, "col"))
     term = term.reshape(child_rows, row_count, block_size, local_cols)
     term = jnp.transpose(term, (1, 0, 2, 3)).reshape(
         row_count * child_rows * block_size, local_cols

time: 627 us -> 710 us (1.13)
  waiting for transfers between devices: 468 us -> 519 us
  local copies, waits for them, and re-layouts: 54.7 us -> 81.9 us
    ppermute x0 -> x7, waiting for transfers between devices: none -> 140 us  [the longest x4 140 us: convert_field_up(): answer = ppermute(answer, link_axis, so_far_all)]
    all_gather x1 -> x0, waiting for transfers between devices: 88 us -> none  [local(): lax.all_gather(product_blocks, 'col', axis=3, tiled=True)]
    dynamic_update_slice x0 -> x8, local copies, waits for them, and re-layouts: none -> 17.8 us  [the longest x4 8.9 us: convert_field_up(): lax.dynamic_update_slice_in_dim(x_next, answer, (spare - c) % a_now * t1,...]
  transfers between devices with their start and end apart: 4 -> 10, of which waited for: 4 -> 7; matrix products, arithmetic and copies ran while one was open for 2% -> 5% of each run, Pallas kernels for 0% -> 0%
where the time goes in v1:
time: 710 us; the launch traced here: 709 us
  waiting for transfers between devices  519 us (73%)
  matrix products  83.9 us (12%)
  local copies, waits for them, and re-layouts  81.9 us (12%)
  between operations  13.2 us (2%)
    all_gather x1, waiting for transfers between devices, local(): panel_all = lax.all_gather(masked, 'row', axis=1, tiled=True)  152 us
    reduce_scatter x1, waiting for transfers between devices, local(): summed = lax.psum_scatter(term, 'row', scatter_dimension=0, tiled=True)  144 us
    ppermute x4, waiting for transfers between devices, convert_field_up(): answer = ppermute(answer, link_axis, so_far_all)  140 us
    all_gather x1, waiting for transfers between devices, local(): segment = lax.all_gather(ancestor_pivot, 'col', axis=3, tiled=True)  82.6 us
    dot_general x1, matrix products, local(): jnp.einsum('kcl,cln->kn', weights, panel_split, precision=lax.Precision.H...  54.8 us
    dot_general x1, matrix products, column_term(): jnp.einsum('kcl,kn->cln', shaped, stationary, precision=lax.Precision.HIG...  29.1 us
    reshape x1, local copies, waits for them, and re-layouts, column_term(): shaped = piece.reshape(local_rows, piece.shape[2], piece.shape[3])  18.2 us
    all_gather x1, local copies, waits for them, and re-layouts, local(): segment = lax.all_gather(ancestor_pivot, 'col', axis=3, tiled=True)  15.3 us
  transfers between devices with their start and end apart: 10, of which 7 were waited for; matrix products, arithmetic and copies ran while one was open for 5% of the time, Pallas kernels for 0%

profile of v1, /device:TPU:0, one launch (start us, length us, event | category | flops | bytes accessed | tf_op | source)
XLA Modules:
  0.0 709.4 jit_solution(11212051598143494029)
XLA Ops:
  6.5 0.0 all-gather.3.cloned.1.call-start
  6.5 0.8 reshape.28
  7.4 0.1 constant_dynamic-slice_fusion
  7.4 0.1 copy.15
  7.6 0.1 copy.9
  7.6 3.4 broadcast_multiply_fusion
  11.0 0.0 all-gather.3.cloned.1.call-update
  11.0 0.0 all-gather.5.cloned.1.call-start
  11.1 0.7 all-gather.5.cloned.1.call-update
  11.8 0.0 reduce-scatter.2.cloned.1.call-start
  11.8 151.7 %all-gather.3.cloned.1.call-done = f32[8,512,4,128]{3,2,1,0:T(4,128)} async-done(((f32[8,128,4,128]{3,2,1,0:T(4,128)}), f32[8,512,4,128]{3,2,1,0:T(4,128)}) %all-gather.3.cloned.1.call-update) | async-done | bytes 8388624 | tf_op jit(solution)/shard_map/all_gather | solution.py:36
  163.5 10.5 %reshape.29 = f32[4,1024,512]{2,1,0:T(8,128)} reshape(f32[8,512,4,128]{3,2,1,0:T(4,128)} %all-gather.3.cloned.1.call-done) | data formatting | bytes 16777216 | tf_op jit(solution)/shard_map/reshape | solution.py:37
  174.1 82.6 %all-gather.5.cloned.1.call-done = f32[8,128,4,1024]{3,2,1,0:T(4,128)} async-done(((f32[8,128,4,128]{3,2,1,0:T(4,128)}), f32[8,128,4,1024]{3,2,1,0:T(4,128)}) %all-gather.5.cloned.1.call-update) | async-done | bytes 16777232 | tf_op jit(solution)/shard_map/all_gather | solution.py:38
  256.6 0.0 copy-start.1
  256.6 15.3 %copy.10 = f32[8,128,4,1024]{3,1,0,2:T(8,128)S(1)} copy(f32[8,128,4,1024]{3,2,1,0:T(4,128)} %all-gather.5.cloned.1.call-done) | data formatting | bytes 33554432 | tf_op jit(solution)/shard_map/all_gather | solution.py:38
  272.0 0.0 copy-done.1
  272.0 0.0 copy-start
  272.0 54.8 %convolution_bitcast_fusion.1 = f32[64,8,8,128]{3,1,2,0:T(8,128)S(1)} fusion(f32[4,1024,512]{2,1,0:T(8,128)S(1)} %copy-done.1, f32[1024,4,1024]{2,0,1:T(8,128)S(1)} %bitcast.29), kind=kOutput, calls=%fused_computation.2 | convolution fusion | flops 25769803776 | bytes 27262976 | tf_op jit(solution)/shard_map/kcl,cln->kn/dot_general | solution.py:41
  326.9 0.5 copy.16
  327.3 0.0 copy-start.2
  327.3 0.3 collective-permute-start
  327.6 1.0 copy-done.2
  328.6 1.4 collective-permute-start.1
  330.0 45.3 %collective-permute-done = f32[8,128,4,128]{1,0,3,2:T(8,128)S(1)} collective-permute-done((f32[8,128,4,128]{1,0,3,2:T(8,128)S(1)}, f32[8,128,4,128]{1,0,3,2:T(8,128)S(1)}, u32[]{:S(2)}, u32[]{:S(2)}) %collective-permute-start) | collective-permute-done | bytes 2097184 | tf_op jit(solution)/shard_map/ppermute | solution.py:59
  375.4 0.0 copy-start.4
  375.4 0.0 collective-permute-start.2
  375.4 0.0 collective-permute-done.1
  375.4 1.3 copy-done.4
  376.7 0.0 copy-start.6
  376.7 1.4 collective-permute-start.3
  378.1 46.1 %collective-permute-done.2 = f32[8,128,4,128]{1,0,3,2:T(8,128)S(1)} collective-permute-done((f32[8,128,4,128]{1,0,3,2:T(8,128)S(1)}, f32[8,128,4,128]{1,0,3,2:T(8,128)S(1)}, u32[]{:S(2)}, u32[]{:S(2)}) %collective-permute-start.2) | collective-permute-done | bytes 2097184 | tf_op jit(solution)/shard_map/ppermute | solution.py:59
  424.2 0.0 copy-done.6
  424.2 0.0 copy-start.8
  424.2 0.0 collective-permute-start.4
  424.2 0.0 collective-permute-done.3
  424.2 1.4 copy-done.8
  425.5 1.3 collective-permute-start.5
  426.8 45.7 %collective-permute-done.4 = f32[8,128,4,128]{1,0,3,2:T(8,128)} collective-permute-done((f32[8,128,4,128]{1,0,3,2:T(8,128)S(1)}, f32[8,128,4,128]{1,0,3,2:T(8,128)}, u32[]{:S(2)}, u32[]{:S(2)}) %collective-permute-start.4) | collective-permute-done | bytes 2097184 | tf_op jit(solution)/shard_map/ppermute | solution.py:59
  472.5 0.0 collective-permute-start.6
  472.5 0.0 copy-done
  472.5 1.8 reshape.37
  474.3 6.8 broadcast_in_dim.4
  481.1 0.0 copy-done.3
  481.1 1.4 constant_dynamic-update-slice_fusion.7
  482.6 0.0 copy-done.5
  482.6 1.5 constant_dynamic-update-slice_fusion.6
  484.1 0.0 copy-done.7
  484.1 1.4 constant_dynamic-update-slice_fusion.5
  485.5 0.0 copy-done.9
  485.5 1.4 constant_dynamic-update-slice_fusion.4
  486.9 3.0 constant_dynamic-update-slice_fusion.3
  489.9 3.0 constant_dynamic-update-slice_fusion.2
  492.9 0.0 collective-permute-done.5
  492.9 3.0 constant_dynamic-update-slice_fusion.1
  496.0 3.2 collective-permute-done.6
  499.1 3.0 constant_dynamic-update-slice_fusion
  502.1 18.2 %reshape.32 = f32[1024,4,1024]{0,2,1:T(8,128)} reshape(f32[8,128,4,1024]{1,0,3,2:T(8,128)} %constant_dynamic-update-slice_fusion) | data formatting | bytes 33554432 | tf_op jit(solution)/shard_map/reshape | solution.py:9
  520.3 0.0 copy-done.10
  520.3 29.1 %convolution_bitcast_fusion = f32[4,8,128,512]{3,2,0,1:T(8,128)S(1)} fusion(f32[8,4,128,1024]{3,2,1,0:T(8,128)} %bitcast.30, f32[1024,512,1,1]{1,0,2,3:T(8,128)S(1)} %copy-done.10), kind=kOutput, calls=%fused_computation | convolution fusion | flops 25769803776 | bytes 27262976 | tf_op jit(solution)/shard_map/kcl,kn->cln/dot_general | solution.py:10
  549.4 4.3 copy.12
  553.6 0.0 reduce-scatter.2.cloned.1.call-update
  553.6 143.9 %reduce-scatter.2.cloned.1.call-done = f32[1024,512]{1,0:T(8,128)} async-done(((f32[4096,512]{1,0:T(8,128)}), f32[1024,512]{1,0:T(8,128)}) %reduce-scatter.2.cloned.1.call-update) | async-done | bytes 2097168 | tf_op jit(solution)/shard_map/reduce_scatter | solution.py:75
  697.5 1.9 reshape.35
  699.5 3.5 add.96
  (6 shorter events, 0.0 us)
Async XLA Ops:
  6.5 157.0 %all-gather.3.cloned.1.call-start = ((), (), s32[]{:S(2)}) async-start(), calls=%async_computation.1 | async-start | bytes 10485760 | tf_op jit(solution)/shard_map/all_gather | solution.py:36
  11.0 245.6 %all-gather.5.cloned.1.call-start = ((), (), s32[]{:S(2)}) async-start(), calls=%async_computation.2 | async-start | bytes 18874368 | tf_op jit(solution)/shard_map/all_gather | solution.py:38
  11.8 685.7 %reduce-scatter.2.cloned.1.call-start = ((), (), s32[]{:S(2)}) async-start(), calls=%async_computation.3 | async-start | bytes 10485760 | tf_op jit(solution)/shard_map/reduce_scatter | solution.py:75
  256.6 15.4 %copy-start.1 = (f32[4,1024,512]{2,1,0:T(8,128)S(1)}, f32[4,1024,512]{2,1,0:T(8,128)}, u32[]{:S(2)}) copy-start(f32[4,1024,512]{2,1,0:T(8,128)} %reshape.29) | copy-start | bytes 25165828
  272.0 200.5 %copy-start = (f32[8,128,4,128]{3,2,1,0:T(4,128)S(1)}, f32[8,128,4,128]{3,2,1,0:T(4,128)}, u32[]{:S(2)}) copy-start(f32[8,128,4,128]{3,2,1,0:T(4,128)} %broadcast_multiply_fusion) | copy-start | bytes 6291460
  327.3 1.3 copy-start.2
  327.3 48.0 %collective-permute-start = (f32[8,128,4,128]{1,0,3,2:T(8,128)S(1)}, f32[8,128,4,128]{1,0,3,2:T(8,128)S(1)}, u32[]{:S(2)}, u32[]{:S(2)}) collective-permute-start(f32[8,128,4,128]{1,0,3,2:T(8,128)S(1)} %bitcast.31), channel_id=1, source_target_pairs={{0,1},{1,2},{2,3},{3,4},{4,5},{5,6},{6,7},{7,0},{8,9},{9,10},{10,1... | collective-permute-start | bytes 6291464 | tf_op jit(solution)/shard_map/ppermute | solution.py:59
  328.6 46.7 %collective-permute-start.1 = (f32[8,128,4,128]{1,0,3,2:T(8,128)S(1)}, f32[8,128,4,128]{1,0,3,2:T(8,128)S(1)}, u32[]{:S(2)}, u32[]{:S(2)}) collective-permute-start(f32[8,128,4,128]{1,0,3,2:T(8,128)S(1)} %bitcast.32), channel_id=1, source_target_pairs={{0,7},{1,0},{2,1},{3,2},{4,3},{5,4},{6,5},{7,6},{8,15},{9,8},{10,9... | collective-permute-start | bytes 6291464 | tf_op jit(solution)/shard_map/ppermute | solution.py:64
  375.4 1.3 copy-start.4
  375.4 48.8 %collective-permute-start.2 = (f32[8,128,4,128]{1,0,3,2:T(8,128)S(1)}, f32[8,128,4,128]{1,0,3,2:T(8,128)S(1)}, u32[]{:S(2)}, u32[]{:S(2)}) collective-permute-start(f32[8,128,4,128]{1,0,3,2:T(8,128)S(1)} %collective-permute-done), channel_id=1, source_target_pairs={{0,1},{1,2},{2,3},{3,4},{4,5},{5,6},{6,7},{7,0},{8,9},{9,10},{10,1... | collective-permute-start | bytes 6291464 | tf_op jit(solution)/shard_map/ppermute | solution.py:59
  376.7 47.5 %copy-start.6 = (f32[8,128,4,128]{1,0,3,2:T(8,128)}, f32[8,128,4,128]{1,0,3,2:T(8,128)S(1)}, u32[]{:S(2)}) copy-start(f32[8,128,4,128]{1,0,3,2:T(8,128)S(1)} %collective-permute-done.1) | copy-start | bytes 6291460
  376.7 47.5 %collective-permute-start.3 = (f32[8,128,4,128]{1,0,3,2:T(8,128)S(1)}, f32[8,128,4,128]{1,0,3,2:T(8,128)}, u32[]{:S(2)}, u32[]{:S(2)}) collective-permute-start(f32[8,128,4,128]{1,0,3,2:T(8,128)S(1)} %collective-permute-done.1), channel_id=1, source_target_pairs={{0,7},{1,0},{2,1},{3,2},{4,3},{5,4},{6,5},{7,6},{8,15},{9,8},{10,9... | collective-permute-start | bytes 6291464 | tf_op jit(solution)/shard_map/ppermute | solution.py:64
  424.2 1.4 copy-start.8
  424.2 48.3 %collective-permute-start.4 = (f32[8,128,4,128]{1,0,3,2:T(8,128)S(1)}, f32[8,128,4,128]{1,0,3,2:T(8,128)}, u32[]{:S(2)}, u32[]{:S(2)}) collective-permute-start(f32[8,128,4,128]{1,0,3,2:T(8,128)S(1)} %collective-permute-done.2), channel_id=1, source_target_pairs={{0,1},{1,2},{2,3},{3,4},{4,5},{5,6},{6,7},{7,0},{8,9},{9,10},{10,1... | collective-permute-start | bytes 6291464 | tf_op jit(solution)/shard_map/ppermute | solution.py:59
  425.5 67.4 %collective-permute-start.5 = (f32[8,128,4,128]{1,0,3,2:T(8,128)}, f32[8,128,4,128]{1,0,3,2:T(8,128)}, u32[]{:S(2)}, u32[]{:S(2)}) collective-permute-start(f32[8,128,4,128]{1,0,3,2:T(8,128)} %collective-permute-done.3), channel_id=1, source_target_pairs={{0,7},{1,0},{2,1},{3,2},{4,3},{5,4},{6,5},{7,6},{8,15},{9,8},{10,9... | collective-permute-start | bytes 6291464 | tf_op jit(solution)/shard_map/ppermute | solution.py:64
  472.5 26.7 %collective-permute-start.6 = (f32[8,128,4,128]{1,0,3,2:T(8,128)}, f32[8,128,4,128]{1,0,3,2:T(8,128)}, u32[]{:S(2)}, u32[]{:S(2)}) collective-permute-start(f32[8,128,4,128]{1,0,3,2:T(8,128)} %collective-permute-done.4), channel_id=1, source_target_pairs={{0,1},{1,2},{2,3},{3,4},{4,5},{5,6},{6,7},{7,0},{8,9},{9,10},{10,1... | collective-permute-start | bytes 6291464 | tf_op jit(solution)/shard_map/ppermute | solution.py:59
  474.3 6.8 copy-start.3
  474.3 8.3 %copy-start.5 = (f32[8,128,4,128]{1,0,3,2:T(8,128)S(1)}, f32[8,128,4,128]{1,0,3,2:T(8,128)}, u32[]{:S(2)}) copy-start(f32[8,128,4,128]{1,0,3,2:T(8,128)} %copy-done.4) | copy-start | bytes 6291460
  481.1 2.9 copy-start.7
  481.1 4.4 copy-start.9
  502.1 18.2 %copy-start.10 = (f32[1024,512,1,1]{1,0,2,3:T(8,128)S(1)}, f32[1024,512,1,1]{1,0,2,3:T(8,128)}, u32[]{:S(2)}) copy-start(f32[1024,512,1,1]{1,0,2,3:T(8,128)} %reshape.37) | copy-start | bytes 6291460
Sparse Core Ops, SparseCore 0:
  11.1 152.3 all-gather.2
  165.4 91.1 all-gather.4
  553.8 143.7 reduce-scatter.1
